TPU v7x, 512 devices: a whole 4x8x8 slice. The times are simulated.
512 devices in a mesh: vol: 64 (over z, x, y_hi), path: 8 (over y_lo, core).
Axes of the slice: x: 4, y: 8 (y_hi: 2, y_lo: 4; y = y_hi * 4 + y_lo), z: 8, core: 2. Of those that a mesh axis runs over, the one named last changes fastest.
Arguments:
- factors: bfloat16 [16, 8192], P(None, 'path'), may hold values from -6 to 6
- payoff: float32 [4, 8192], P(None, 'path'), may hold values from -6 to 6
- terminal: float32 [64, 8192], P('vol', 'path'), may hold values from 0.5 to 4
- decisions: int32 [3, 64, 8192], P(None, 'vol', 'path'), may hold values 0 or 1
- level_range: int32 [4, 2], replicated, may hold values from 1 to 63, as said below
- w_in_master: float32 [64, 16, 1024], P('vol'), may hold values from -1.5 to 1.5
- w_mid_master: float32 [64, 1024, 1024], P('vol', 'path'), may hold values from -0.1875 to 0.1875
- vec_master: float32 [64, 3, 1024], P('vol'), may hold values from -0.6 to 0.6
- w_in_copy: bfloat16 [64, 16, 1024], P('vol'), may hold values from -1.5 to 1.5
- w_mid_copy: bfloat16 [64, 1024, 1024], P('vol', 'path'), may hold values from -0.1875 to 0.1875
- mom_in: float32 [64, 16, 1024], P('vol'), may hold values from -0.6 to 0.6
- mom_mid: float32 [64, 1024, 1024], P('vol', 'path'), may hold values from -0.6 to 0.6
- mom_vec: float32 [64, 3, 1024], P('vol'), may hold values from -0.6 to 0.6
Outputs:
- level_value: float32 [64], P('vol')
- new_w_in: float32 [64, 16, 1024], P('vol')
- new_w_mid: float32 [64, 1024, 1024], P('vol', 'path')
- new_vec: float32 [64, 3, 1024], P('vol')
- new_mom_in: float32 [64, 16, 1024], P('vol')
- new_mom_mid: float32 [64, 1024, 1024], P('vol', 'path')
- new_mom_vec: float32 [64, 3, 1024], P('vol')
- new_in_copy: bfloat16 [64, 16, 1024], P('vol')
- new_mid_copy: bfloat16 [64, 1024, 1024], P('vol', 'path')
Inputs may be any that keep to these rules, and one draw needn't show every extreme that they name: At every date level_range[s, 0] <= level_range[s, 1] and level 0 lies below the range; at dates 1 to 3 the range starts at level 1; at date 0 the range holds exactly 32 levels.
All inputs are finite; a program needn't handle non-finite values. No bound on the sum of `decisions` on one device may be relied on, other than what follows from the above.
Results may differ from a plain program's by a relative error of at most 0.015.
Values may be sent and summed in bfloat16 or wider, within the bound.
A program may use at most 64 MiB of HBM per device.

v0:
```python
import jax
import jax.numpy as jnp
from jax import lax
from jax.sharding import PartitionSpec as P

MOMENTUM = 0.9
STEP_SIZE = 0.01


def from_behind(value, axis, steps):
    count = lax.axis_size(axis)
    leading, last = (max(0, -steps), min(count, count - steps))
    return lax.ppermute(value, axis, [(source, source + steps) for source in range(leading, last)])


def copy_for_each(value, axis):
    length = lax.axis_size(axis)
    return lax.all_to_all(
        jnp.broadcast_to(value[None], (length, *value.shape)), axis, 0, 0, tiled=True
    )


def of_everyone(value, axis):
    everything = copy_for_each(value, axis)
    return jnp.sum(everything, axis=0)


def together(arrays, axis):
    line, at, outs = (jnp.concatenate([a.reshape(-1) for a in arrays]), 0, [])
    so_far = of_everyone(line, axis)
    for a in arrays:
        outs.append(so_far[at : at + a.size].reshape(a.shape))
        at += a.size
    return tuple(outs)


def silu_parts(preact):
    squash = jax.nn.sigmoid(preact)
    return (preact * squash, squash * (1.0 + preact * (1.0 - squash)))


def network_pass(w_first, w_second, vectors, features, gain_row, enabled):
    pre_one = (
        lax.dot_general(
            features, w_first, (((0,), (0,)), ((), ())), preferred_element_type=jnp.float32
        )
        + vectors[0]
    )
    act_one, slope_one = silu_parts(pre_one)
    hidden_one = act_one.astype(jnp.bfloat16)
    pre_two = jnp.dot(hidden_one, w_second, preferred_element_type=jnp.float32) + vectors[1]
    act_two, slope_two = silu_parts(pre_two)
    hidden_two = act_two.astype(jnp.bfloat16)
    logits = jnp.sum(hidden_two.astype(jnp.float32) * vectors[2], axis=1)
    chance = jax.nn.sigmoid(logits)
    d_logit = jnp.where(enabled, -gain_row * chance * (1.0 - chance), 0.0)
    d_head = jnp.sum(d_logit[:, None] * hidden_two.astype(jnp.float32), axis=0)
    d_pre_two = d_logit[:, None] * vectors[2] * slope_two
    d_bias_two = jnp.sum(d_pre_two, axis=0)
    d_two_low = d_pre_two.astype(jnp.bfloat16)
    d_hidden_one = lax.dot_general(
        d_two_low, w_second, (((1,), (1,)), ((), ())), preferred_element_type=jnp.float32
    )
    d_pre_one = d_hidden_one * slope_one
    d_bias_one = jnp.sum(d_pre_one, axis=0)
    d_first = jnp.dot(features, d_pre_one.astype(jnp.bfloat16), preferred_element_type=jnp.float32)
    d_vectors = jnp.stack([d_bias_one, d_bias_two, d_head])
    value_sum = jnp.where(enabled, jnp.sum(chance * gain_row), 0.0)
    return (hidden_one, d_two_low, d_first, d_vectors, value_sum)


def row_product(hidden_one, d_two_low):
    return lax.dot_general(
        hidden_one, d_two_low, (((0,), (0,)), ((), ())), preferred_element_type=jnp.float32
    )


def lower_neighbour(values):
    return from_behind(values, "vol", 1)


def full_rows(row_shard):
    return lax.all_gather(row_shard, "path", axis=0, tiled=True)


def shards(
    factors,
    payoff,
    terminal,
    decisions,
    level_range,
    w_in_master,
    w_mid_master,
    vec_master,
    w_in_copy,
    w_mid_copy,
    mom_in,
    mom_mid,
    mom_vec,
):
    level_here = lax.axis_index("vol")
    dates = payoff.shape[0]
    paths_here = payoff.shape[1]
    carry_value = terminal[0]
    for date_index in range(dates - 1, 0, -1):
        lower_row = lower_neighbour(carry_value)
        lower_end = level_range[date_index, 0]
        upper_end = level_range[date_index, 1]
        inside = jnp.logical_and(level_here >= lower_end, level_here <= upper_end)
        taken_now = jnp.where(
            level_here > upper_end,
            1.0,
            jnp.where(inside, decisions[date_index - 1, 0].astype(jnp.float32), 0.0),
        )
        carry_value = taken_now * (payoff[date_index] + lower_row) + (1.0 - taken_now) * carry_value
    lower_row = lower_neighbour(carry_value)
    gain_row = payoff[0] + lower_row - carry_value
    low_now = level_range[0, 0]
    high_now = level_range[0, 1]
    active = jnp.logical_and(level_here >= low_now, level_here <= high_now)
    forced = jnp.where(level_here > high_now, 1.0, 0.0)
    first_copy = w_in_copy[0]
    vectors = vec_master[0]
    second_full = full_rows(w_mid_copy[0])
    hidden_one, d_two_low, d_first, d_vectors, value_sum = network_pass(
        first_copy, second_full, vectors, factors, gain_row, active
    )
    mid_grad = lax.psum_scatter(
        row_product(hidden_one, d_two_low).astype(jnp.bfloat16),
        "path",
        scatter_dimension=0,
        tiled=True,
    ).astype(jnp.float32)
    value_local = jnp.where(active, value_sum, forced * jnp.sum(gain_row)) + jnp.sum(carry_value)
    d_first, d_vectors, value_local = together((d_first, d_vectors, value_local), "path")
    paths_total = paths_here * lax.axis_size("path")
    level_value = (value_local / paths_total)[None]
    new_mom_in = MOMENTUM * mom_in + d_first[None]
    new_mom_mid = MOMENTUM * mom_mid + mid_grad[None]
    new_mom_vec = MOMENTUM * mom_vec + d_vectors[None]
    new_w_in = w_in_master - STEP_SIZE * new_mom_in
    new_w_mid = w_mid_master - STEP_SIZE * new_mom_mid
    new_vec = vec_master - STEP_SIZE * new_mom_vec
    return (
        level_value,
        new_w_in,
        new_w_mid,
        new_vec,
        new_mom_in,
        new_mom_mid,
        new_mom_vec,
        new_w_in.astype(jnp.bfloat16),
        new_w_mid.astype(jnp.bfloat16),
    )


def solution(mesh):
    in_specs = (
        P(None, "path"),
        P(None, "path"),
        P("vol", "path"),
        P(None, "vol", "path"),
        P(),
        P("vol", None, None),
        P("vol", "path", None),
        P("vol", None, None),
        P("vol", None, None),
        P("vol", "path", None),
        P("vol", None, None),
        P("vol", "path", None),
        P("vol", None, None),
    )
    out_specs = (
        P("vol"),
        P("vol", None, None),
        P("vol", "path", None),
        P("vol", None, None),
        P("vol", None, None),
        P("vol", "path", None),
        P("vol", None, None),
        P("vol", None, None),
        P("vol", "path", None),
    )
    return jax.shard_map(shards, mesh=mesh, in_specs=in_specs, out_specs=out_specs, check_vma=False)
```

profile of v0, /device:TPU:9, one launch (start us, length us, event | category | flops | bytes accessed | tf_op | source)
XLA Modules:
  0.0 136.0 jit_solution(5936669052276414330)
XLA Ops:
  7.2 0.0 copy-start
  7.2 0.0 all-gather.3.cloned.1.call-start
  7.2 0.7 all-gather.3.cloned.1.call-update
  7.9 0.0 reduce-scatter.2.cloned.1.call-start
  8.0 6.6 %collective-permute-start = (f32[1024]{0:T(1024)}, f32[1024]{0:T(1024)S(1)}, u32[]{:S(2)}, u32[]{:S(2)}) collective-permute-start(f32[1024]{0:T(1024)} %bitcast.66), channel_id=1, source_target_pairs={{0,8},{8,16},{16,24},{24,32},{32,40},{40,48},{48,56},{56,64},{64,7... | collective-permute-start | bytes 12296 | tf_op jit(solution)/shard_map/ppermute | solution.py:13
  14.5 1.6 %fusion.21 = (s32[1,1]{0,1:T(1,128)}, s32[1,1]{0,1:T(1,128)}, s32[1,1]{0,1:T(1,128)}, s32[1,1]{0,1:T(1,128)}, s32[1,1]{0,1:T(1,128)}, /*index=5*/s32[1,1]{0,1:T(1,128)}, s32[1,1]{0,1:T(1,128)}, s32[1,1]{0,1:T(1,128)}) fusion(s32[4,2]{0,1:T(2,128)} %param.17), kind=kLoop, calls=%fused_computation.49 | loop fusion | bytes 64 | tf_op jit(solution)/shard_map/slice | solution.py:107
  22.0 0.9 fusion.19
  22.9 0.7 broadcast_select_fusion.5
  23.6 0.7 multiply_add_fusion.4
  24.3 3.6 %collective-permute-start.1 = (f32[1024]{0:T(1024)S(1)}, f32[1024]{0:T(1024)S(1)}, u32[]{:S(2)}, u32[]{:S(2)}) collective-permute-start(f32[1024]{0:T(1024)S(1)} %multiply_add_fusion.4), channel_id=1, source_target_pairs={{0,8},{8,16},{16,24},{24,32},{32,40},{40,48},{48,56},{56,64},{64,7... | collective-permute-start | bytes 12296 | tf_op jit(solution)/shard_map/ppermute | solution.py:13
  27.9 3.4 %fusion.12 = f32[1024,1024]{1,0:T(8,128)} fusion(bf16[16,1024]{1,0:T(8,128)(2,1)S(1)} %copy-done, bf16[1,16,1024]{2,1,0:T(8,128)(2,1)} %param.21), kind=kOutput, calls=%fused_computation.24 | convolution fusion | flops 33554432 | bytes 4259840 | tf_op jit(solution)/shard_map/dot_general | solution.py:44
  31.3 6.6 %collective-permute-start.2 = (f32[1024]{0:T(1024)S(1)}, f32[1024]{0:T(1024)S(1)}, u32[]{:S(2)}, u32[]{:S(2)}) collective-permute-start(f32[1024]{0:T(1024)S(1)} %multiply_add_fusion.3), channel_id=1, source_target_pairs={{0,8},{8,16},{16,24},{24,32},{32,40},{40,48},{48,56},{56,64},{64,7... | collective-permute-start | bytes 12296 | tf_op jit(solution)/shard_map/ppermute | solution.py:13
  39.9 0.6 fusion.18
  40.5 6.5 %collective-permute-start.3 = (f32[1024]{0:T(1024)S(1)}, f32[1024]{0:T(1024)S(1)}, u32[]{:S(2)}, u32[]{:S(2)}) collective-permute-start(f32[1024]{0:T(1024)S(1)} %get-tuple-element.24), channel_id=1, source_target_pairs={{0,8},{8,16},{16,24},{24,32},{32,40},{40,48},{48,56},{56,64},{64,7... | collective-permute-start | bytes 12296 | tf_op jit(solution)/shard_map/ppermute | solution.py:13
  46.9 4.7 %all-gather.3.cloned.1.call-done = bf16[1,1024,1024]{2,1,0:T(8,128)(2,1)} async-done(((bf16[1,128,1024]{2,1,0:T(8,128)(2,1)}), bf16[1,1024,1024]{2,1,0:T(8,128)(2,1)}) %all-gather.3.cloned.1.call-update) | async-done | bytes 2097168 | tf_op jit(solution)/shard_map/all_gather | solution.py:83
  51.6 5.9 %fusion = (f32[1024]{0:T(1024)S(1)}, bf16[1024,1024]{1,0:T(8,128)(2,1)S(1)}, f32[1024,1024]{1,0:T(8,128)S(1)}) fusion(f32[1024]{0:T(1024)S(1)} %bitcast.62, f32[1024]{0:T(1024)S(1)} %bitcast.58, bf16[1,1024,1024]{2,1,0:T(8,128)(2,1)} %all-gather.3.cloned.1.call-done, f32[1024,1024]{1,0:T(8,128)} %fusion.12, f32[1024]{0:T(1024)S(1)} %bitcast.69), kind=kOutput, calls=%fused_computation.2 | convolution fusion | flops 2163211264 | bytes 12599296 | tf_op jit(solution)/shard_map/dot_general | solution.py:51
  57.6 1.9 %copy-done.2 = f32[1024,1024]{1,0:T(8,128)} copy-done((f32[1024,1024]{1,0:T(8,128)}, f32[1024,1024]{1,0:T(8,128)S(1)}, u32[]{:S(2)}) %copy-start.2) | copy-done | bytes 4194328
  59.5 5.2 %convolution_convert_fusion = bf16[1024,1024]{1,0:T(8,128)(2,1)} fusion(f32[1024,1024]{1,0:T(8,128)S(1)} %copy-done.1, f32[1024]{0:T(1024)S(1)} %bitcast.70, f32[1024,1024]{1,0:T(8,128)S(1)} %get-tuple-element.45, f32[1024]{0:T(1024)S(1)} %get-tuple-element.21, f32[1024]{0:T(1024)S(1)} %bitcast.63, f32[1024]{0:T(1024)S(1)} %bitcast.59), kind=kOutput, calls=%fused_computation.15 | convolution fusion | flops 2166358016 | bytes 10502144 | tf_op jit(solution)/shard_map/dot_general | solution.py:73
  64.7 0.0 reduce-scatter.2.cloned.1.call-update
  64.8 4.0 %fusion.14 = (f32[1024]{0:T(1024)S(1)}, f32[1024]{0:T(1024)S(1)}) fusion(f32[1024,1024]{1,0:T(8,128)} %copy-done.2, f32[1024]{0:T(1024)S(1)} %bitcast.60, f32[1024]{0:T(1024)S(1)} %bitcast.64, f32[1024]{0:T(1024)S(1)} %get-tuple-element.21, bf16[1024,1024]{1,0:T(8,128)(2,1)S(1)} %get-tuple-element.26), kind=kLoop, calls=%fused_computation.42 | loop fusion | flops 14678016 | bytes 6311936 | tf_op jit(solution)/shard_map/reduce_sum | solution.py:59
  68.8 0.6 fusion.15
  70.0 7.2 %fusion.22 = (f32[1024]{0:T(1024)S(1)}, bf16[1024,1024]{1,0:T(8,128)(2,1)S(1)}) fusion(f32[1024,1024]{1,0:T(8,128)} %fusion.12, f32[1024]{0:T(1024)S(1)} %bitcast.71, bf16[1,1024,1024]{2,1,0:T(8,128)(2,1)} %all-gather.3.cloned.1.call-done, f32[1024,1024]{1,0:T(8,128)} %copy-done.2, f32[1024]{0:T(1024)S(1)} %bitcast.61, f32[1024]{0:T(1024)S(1)} %bitcast.65, ...), kind=kOutput, calls=%fused_computation.50 | convolution fusion | flops 2170551296 | bytes 12603392 | tf_op jit(solution)/shard_map/dot_general | solution.py:61
  77.2 0.0 copy-start.5
  77.3 0.4 fusion.7
  79.0 0.3 broadcast_in_dim.36
  79.4 33.8 %all_to_all.6 = f32[8,1,19457]{2,1,0:T(1,128)S(1)} all-to-all(f32[8,1,19457]{2,1,0:T(1,128)S(1)} %broadcast_in_dim.36), channel_id=1, replica_groups=mesh['vol'=64,'path'=8] {'path'}, dimensions={0} | all-to-all | bytes 1245248 | tf_op jit(solution)/shard_map/all_to_all | solution.py:18
  113.2 0.5 reduce_sum.79
  113.6 0.5 slice.88
  114.8 0.6 multiply_subtract_fusion.2
  115.5 0.7 fusion.17
  116.2 9.7 %reduce-scatter.2.cloned.1.call-done = bf16[128,1024]{1,0:T(8,128)(2,1)} async-done(((bf16[1024,1024]{1,0:T(8,128)(2,1)}), bf16[128,1024]{1,0:T(8,128)(2,1)}) %reduce-scatter.2.cloned.1.call-update) | async-done | bytes 262160 | tf_op jit(solution)/shard_map/reduce_scatter | solution.py:128
  125.9 2.1 %fusion.16 = (bf16[1,128,1024]{2,1,0:T(8,128)(2,1)}, f32[1,128,1024]{2,1,0:T(8,128)}, f32[1,128,1024]{2,1,0:T(8,128)}) fusion(f32[1,128,1024]{2,1,0:T(8,128)S(1)} %copy-done.3, bf16[128,1024]{1,0:T(8,128)(2,1)} %reduce-scatter.2.cloned.1.call-done, f32[1,128,1024]{2,1,0:T(8,128)S(1)} %copy-done.4), kind=kLoop, calls=%fused_computation.44 | loop fusion | flops 786432 | bytes 2621440 | tf_op jit(solution)/shard_map/convert_element_type | solution.py:153
  (29 shorter events, 0.2 us)
Async XLA Ops:
  7.2 20.7 %copy-start = (bf16[16,1024]{1,0:T(8,128)(2,1)S(1)}, bf16[16,1024]{1,0:T(8,128)(2,1)}, u32[]{:S(2)}) copy-start(bf16[16,1024]{1,0:T(8,128)(2,1)} %param.13) | copy-start | bytes 98308
  7.2 30.7 %copy-start.7 = (f32[1,3,1024]{2,0,1:T(1,128)S(1)}, f32[1,3,1024]{2,0,1:T(1,128)}, u32[]{:S(2)}) copy-start(f32[1,3,1024]{2,0,1:T(1,128)} %param.20) | copy-start | bytes 36868
  7.2 44.4 %all-gather.3.cloned.1.call-start = ((), (), s32[]{:S(2)}) async-start(), calls=%async_computation.3 | async-start | bytes 2359296 | tf_op jit(solution)/shard_map/all_gather | solution.py:83
  7.9 117.9 %reduce-scatter.2.cloned.1.call-start = ((), (), s32[]{:S(2)}) async-start(), calls=%async_computation.2 | async-start | bytes 2359296 | tf_op jit(solution)/shard_map/reduce_scatter | solution.py:128
  8.0 15.6 %collective-permute-start = (f32[1024]{0:T(1024)}, f32[1024]{0:T(1024)S(1)}, u32[]{:S(2)}, u32[]{:S(2)}) collective-permute-start(f32[1024]{0:T(1024)} %bitcast.66), channel_id=1, source_target_pairs={{0,8},{8,16},{16,24},{24,32},{32,40},{40,48},{48,56},{56,64},{64,7... | collective-permute-start | bytes 12296 | tf_op jit(solution)/shard_map/ppermute | solution.py:13
  24.3 7.0 %collective-permute-start.1 = (f32[1024]{0:T(1024)S(1)}, f32[1024]{0:T(1024)S(1)}, u32[]{:S(2)}, u32[]{:S(2)}) collective-permute-start(f32[1024]{0:T(1024)S(1)} %multiply_add_fusion.4), channel_id=1, source_target_pairs={{0,8},{8,16},{16,24},{24,32},{32,40},{40,48},{48,56},{56,64},{64,7... | collective-permute-start | bytes 12296 | tf_op jit(solution)/shard_map/ppermute | solution.py:13
  31.3 8.5 %collective-permute-start.2 = (f32[1024]{0:T(1024)S(1)}, f32[1024]{0:T(1024)S(1)}, u32[]{:S(2)}, u32[]{:S(2)}) collective-permute-start(f32[1024]{0:T(1024)S(1)} %multiply_add_fusion.3), channel_id=1, source_target_pairs={{0,8},{8,16},{16,24},{24,32},{32,40},{40,48},{48,56},{56,64},{64,7... | collective-permute-start | bytes 12296 | tf_op jit(solution)/shard_map/ppermute | solution.py:13
  40.5 17.1 %collective-permute-start.3 = (f32[1024]{0:T(1024)S(1)}, f32[1024]{0:T(1024)S(1)}, u32[]{:S(2)}, u32[]{:S(2)}) collective-permute-start(f32[1024]{0:T(1024)S(1)} %get-tuple-element.24), channel_id=1, source_target_pairs={{0,8},{8,16},{16,24},{24,32},{32,40},{40,48},{48,56},{56,64},{64,7... | collective-permute-start | bytes 12296 | tf_op jit(solution)/shard_map/ppermute | solution.py:13
  51.6 7.9 %copy-start.1 = (f32[1024,1024]{1,0:T(8,128)S(1)}, f32[1024,1024]{1,0:T(8,128)}, u32[]{:S(2)}) copy-start(f32[1024,1024]{1,0:T(8,128)} %fusion.12) | copy-start | bytes 12582916
  57.5 2.0 %copy-start.2 = (f32[1024,1024]{1,0:T(8,128)}, f32[1024,1024]{1,0:T(8,128)S(1)}, u32[]{:S(2)}) copy-start(f32[1024,1024]{1,0:T(8,128)S(1)} %get-tuple-element.45) | copy-start | bytes 12582916
  77.2 37.6 %copy-start.8 = (f32[1,3,1024]{2,0,1:T(1,128)S(1)}, f32[1,3,1024]{2,0,1:T(1,128)}, u32[]{:S(2)}) copy-start(f32[1,3,1024]{2,0,1:T(1,128)} %param.25) | copy-start | bytes 36868
  77.2 38.2 %copy-start.5 = (f32[1,16,1024]{2,1,0:T(8,128)S(1)}, f32[1,16,1024]{2,1,0:T(8,128)}, u32[]{:S(2)}) copy-start(f32[1,16,1024]{2,1,0:T(8,128)} %param.18) | copy-start | bytes 196612
  77.2 38.2 %copy-start.6 = (f32[1,16,1024]{2,1,0:T(8,128)S(1)}, f32[1,16,1024]{2,1,0:T(8,128)}, u32[]{:S(2)}) copy-start(f32[1,16,1024]{2,1,0:T(8,128)} %param.23) | copy-start | bytes 196612
  77.3 48.6 %copy-start.3 = (f32[1,128,1024]{2,1,0:T(8,128)S(1)}, f32[1,128,1024]{2,1,0:T(8,128)}, u32[]{:S(2)}) copy-start(f32[1,128,1024]{2,1,0:T(8,128)} %param.19) | copy-start | bytes 1572868
  77.3 48.6 %copy-start.4 = (f32[1,128,1024]{2,1,0:T(8,128)S(1)}, f32[1,128,1024]{2,1,0:T(8,128)}, u32[]{:S(2)}) copy-start(f32[1,128,1024]{2,1,0:T(8,128)} %param.24) | copy-start | bytes 1572868
Sparse Core Ops, SparseCore 0:
  10.1 41.4 all-gather.2
  64.9 60.9 reduce-scatter.1
where the time goes:
time: 137 us; the launch traced here: 136 us
  blocking collectives  33.8 us (25%)
  between operations  25.8 us (19%)
  starting transfers between devices  23.2 us (17%)
  matrix products  22.1 us (16%)
  waiting for transfers between devices  15.1 us (11%)
  other arithmetic  10.6 us (8%)
  local copies, waits for them, and re-layouts  5.35 us (4%)
    all_to_all x1, blocking collectives, copy_for_each(): lax.all_to_all(jnp.broadcast_to(value[None], (length, *value.shape)), axi...  33.8 us
    ppermute x4, starting transfers between devices, from_behind(): lax.ppermute(value, axis, [(source, source + steps) for source in range(l...  23.1 us
    reduce_scatter x1, waiting for transfers between devices, shards(): lax.psum_scatter(row_product(hidden_one, d_two_low).astype(jnp.bfloat16),...  9.72 us
    dot_general x1, matrix products, network_pass(): lax.dot_general(d_two_low, w_second, (((1,), (1,)), ((), ())), preferred_...  7.18 us
    dot_general x1, matrix products, network_pass(): jnp.dot(hidden_one, w_second, preferred_element_type=jnp.float32)  5.92 us
    dot_general x1, matrix products, row_product(): lax.dot_general(hidden_one, d_two_low, (((0,), (0,)), ((), ())), preferre...  5.22 us
    all_gather x1, waiting for transfers between devices, full_rows(): return lax.all_gather(row_shard, 'path', axis=0, tiled=True)  4.7 us
    reduce_sum x1, other arithmetic, network_pass(): d_bias_two = jnp.sum(d_pre_two, axis=0)  3.98 us
  transfers between devices with their start and end apart: 6, of which 2 were waited for; matrix products, arithmetic and copies ran while one was open for 21% of the time, Pallas kernels for 0%

commit v1 on v0

--- a/solution.py
+++ b/solution.py
@@ -80,7 +80,9 @@
 
 
 def full_rows(row_shard):
-    return lax.all_gather(row_shard, "path", axis=0, tiled=True)
+    return jnp.concatenate(
+        lax.all_to_all(jnp.stack([row_shard] * lax.axis_size("path")), "path", 0, 0), axis=0
+    )
 
 
 def shards(

time: 137 us -> 169 us (1.23)
  the two profiles are of different devices: /device:TPU:9 before, /device:TPU:15 now
where the time goes in v1:
time: 169 us
  blocking collectives  46.1 us (27%)
  waiting for transfers between devices  30.2 us (18%)
  starting transfers between devices  26.9 us (16%)
  between operations  25.8 us (15%)
  matrix products  24.3 us (14%)
  other arithmetic  9.43 us (6%)
  local copies, waits for them, and re-layouts  6.09 us (4%)
    all_to_all x1, blocking collectives, copy_for_each(): lax.all_to_all(jnp.broadcast_to(value[None], (length, *value.shape)), axi...  46.1 us
    ppermute x4, starting transfers between devices, from_behind(): lax.ppermute(value, axis, [(source, source + steps) for source in range(l...  21.1 us
    ppermute x4, waiting for transfers between devices, from_behind(): lax.ppermute(value, axis, [(source, source + steps) for source in range(l...  17.9 us
    reduce_scatter x1, waiting for transfers between devices, shards(): lax.psum_scatter(row_product(hidden_one, d_two_low).astype(jnp.bfloat16),...  12.3 us
    dot_general x1, matrix products, network_pass(): lax.dot_general(d_two_low, w_second, (((1,), (1,)), ((), ())), preferred_...  7.5 us
    dot_general x1, matrix products, network_pass(): jnp.dot(hidden_one, w_second, preferred_element_type=jnp.float32)  6.79 us
    all_to_all x1, starting transfers between devices, full_rows(): lax.all_to_all(jnp.stack([row_shard] * lax.axis_size('path')), 'path', 0, 0)  5.77 us
    dot_general x1, matrix products, row_product(): lax.dot_general(hidden_one, d_two_low, (((0,), (0,)), ((), ())), preferre...  5.27 us
  transfers between devices with their start and end apart: 6, of which 4 were waited for; matrix products, arithmetic and copies ran while one was open for 16% of the time, Pallas kernels for 0%

profile of v1, /device:TPU:15, one launch (start us, length us, event | category | flops | bytes accessed | tf_op | source)
XLA Modules:
  0.0 168.9 jit_solution(6287145840256256338)
XLA Ops:
  7.2 0.0 copy-start
  7.2 2.5 %stack.15 = bf16[8,128,1024]{2,1,0:T(8,128)(2,1)} broadcast(bf16[128,1024]{1,0:T(8,128)(2,1)} %bitcast.44), dimensions={1,2} | broadcast | bytes 2359296 | tf_op jit(solution)/shard_map/stack | solution.py:84
  9.8 5.8 %all-to-all-start = ((bf16[8,128,1024]{2,1,0:T(8,128)(2,1)}), bf16[8,128,1024]{2,1,0:T(8,128)(2,1)S(1)}, u32[]{:S(2)}, u32[]{:S(2)}) async-start(bf16[8,128,1024]{2,1,0:T(8,128)(2,1)} %stack.15), calls=%async_computation | async-start | bytes 4194304 | tf_op jit(solution)/shard_map/all_to_all | solution.py:84
  15.6 6.1 %collective-permute-start = (f32[1024]{0:T(1024)S(1)}, f32[1024]{0:T(1024)S(1)}, u32[]{:S(2)}, u32[]{:S(2)}) collective-permute-start(f32[1024]{0:T(1024)S(1)} %bitcast.64), channel_id=1, source_target_pairs={{0,8},{8,16},{16,24},{24,32},{32,40},{40,48},{48,56},{56,64},{64,7... | collective-permute-start | bytes 12296 | tf_op jit(solution)/shard_map/ppermute | solution.py:13
  21.7 0.6 fusion.19
  28.2 12.4 %collective-permute-done = f32[1024]{0:T(1024)S(1)} collective-permute-done((f32[1024]{0:T(1024)S(1)}, f32[1024]{0:T(1024)S(1)}, u32[]{:S(2)}, u32[]{:S(2)}) %collective-permute-start) | collective-permute-done | bytes 4128 | tf_op jit(solution)/shard_map/ppermute | solution.py:13
  40.6 2.9 %collective-permute-start.1 = (f32[1024]{0:T(1024)S(1)}, f32[1024]{0:T(1024)S(1)}, u32[]{:S(2)}, u32[]{:S(2)}) collective-permute-start(f32[1024]{0:T(1024)S(1)} %multiply_add_fusion.4), channel_id=1, source_target_pairs={{0,8},{8,16},{16,24},{24,32},{32,40},{40,48},{48,56},{56,64},{64,7... | collective-permute-start | bytes 12296 | tf_op jit(solution)/shard_map/ppermute | solution.py:13
  43.5 2.7 %fusion.9 = f32[1024,1024]{1,0:T(8,128)} fusion(bf16[16,1024]{1,0:T(8,128)(2,1)S(1)} %copy-done, bf16[1,16,1024]{2,1,0:T(8,128)(2,1)S(1)} %copy-done.8), kind=kOutput, calls=%fused_computation.21 | convolution fusion | flops 33554432 | bytes 4259840 | tf_op jit(solution)/shard_map/dot_general | solution.py:44
  46.1 3.7 %collective-permute-done.1 = f32[1024]{0:T(1024)S(1)} collective-permute-done((f32[1024]{0:T(1024)S(1)}, f32[1024]{0:T(1024)S(1)}, u32[]{:S(2)}, u32[]{:S(2)}) %collective-permute-start.1) | collective-permute-done | bytes 4128 | tf_op jit(solution)/shard_map/ppermute | solution.py:13
  49.9 5.4 %collective-permute-start.2 = (f32[1024]{0:T(1024)S(1)}, f32[1024]{0:T(1024)S(1)}, u32[]{:S(2)}, u32[]{:S(2)}) collective-permute-start(f32[1024]{0:T(1024)S(1)} %multiply_add_fusion.3), channel_id=1, source_target_pairs={{0,8},{8,16},{16,24},{24,32},{32,40},{40,48},{48,56},{56,64},{64,7... | collective-permute-start | bytes 12296 | tf_op jit(solution)/shard_map/ppermute | solution.py:13
  57.2 1.8 %collective-permute-done.2 = f32[1024]{0:T(1024)S(1)} collective-permute-done((f32[1024]{0:T(1024)S(1)}, f32[1024]{0:T(1024)S(1)}, u32[]{:S(2)}, u32[]{:S(2)}) %collective-permute-start.2) | collective-permute-done | bytes 4128 | tf_op jit(solution)/shard_map/ppermute | solution.py:13
  59.0 0.6 fusion.16
  59.6 6.8 %collective-permute-start.3 = (f32[1024]{0:T(1024)S(1)}, f32[1024]{0:T(1024)S(1)}, u32[]{:S(2)}, u32[]{:S(2)}) collective-permute-start(f32[1024]{0:T(1024)S(1)} %get-tuple-element.24), channel_id=1, source_target_pairs={{0,8},{8,16},{16,24},{24,32},{32,40},{40,48},{48,56},{56,64},{64,7... | collective-permute-start | bytes 12296 | tf_op jit(solution)/shard_map/ppermute | solution.py:13
  66.4 0.0 all-to-all-done
  66.5 6.8 %fusion = (f32[1024]{0:T(1024)S(1)}, bf16[1024,1024]{1,0:T(8,128)(2,1)}, f32[1024,1024]{1,0:T(8,128)S(1)}) fusion(f32[1024]{0:T(1024)S(1)} %bitcast.60, f32[1024]{0:T(1024)S(1)} %bitcast.56, bf16[1024,1024]{1,0:T(8,128)(2,1)S(1)} %bitcast.42, f32[1024,1024]{1,0:T(8,128)} %fusion.9, f32[1024]{0:T(1024)S(1)} %bitcast.67), kind=kOutput, calls=%fused_computation.2 | convolution fusion | flops 2163211264 | bytes 12599296 | tf_op jit(solution)/shard_map/dot_general | solution.py:51
  73.3 2.0 %copy-done.2 = f32[1024,1024]{1,0:T(8,128)} copy-done((f32[1024,1024]{1,0:T(8,128)}, f32[1024,1024]{1,0:T(8,128)S(1)}, u32[]{:S(2)}) %copy-start.2) | copy-done | bytes 4194328
  75.2 5.3 %convolution_convert_fusion = bf16[1024,1024]{1,0:T(8,128)(2,1)} fusion(f32[1024,1024]{1,0:T(8,128)S(1)} %copy-done.1, f32[1024]{0:T(1024)S(1)} %bitcast.68, f32[1024,1024]{1,0:T(8,128)S(1)} %get-tuple-element.45, f32[1024]{0:T(1024)S(1)} %get-tuple-element.21, f32[1024]{0:T(1024)S(1)} %bitcast.61, f32[1024]{0:T(1024)S(1)} %bitcast.57), kind=kOutput, calls=%fused_computation.12 | convolution fusion | flops 2166358016 | bytes 10502144 | tf_op jit(solution)/shard_map/dot_general | solution.py:73
  80.5 0.0 reduce-scatter.2.cloned.1.call-update
  80.5 4.2 %fusion.12 = (f32[1024]{0:T(1024)S(1)}, f32[1024]{0:T(1024)S(1)}) fusion(f32[1024,1024]{1,0:T(8,128)} %copy-done.2, f32[1024]{0:T(1024)S(1)} %bitcast.58, f32[1024]{0:T(1024)S(1)} %bitcast.62, f32[1024]{0:T(1024)S(1)} %get-tuple-element.21, bf16[1024,1024]{1,0:T(8,128)(2,1)} %get-tuple-element.26), kind=kLoop, calls=%fused_computation.40 | loop fusion | flops 14678016 | bytes 6311936 | tf_op jit(solution)/shard_map/reduce_sum | solution.py:59
  84.8 0.6 fusion.13
  86.0 7.5 %fusion.20 = (f32[1024]{0:T(1024)S(1)}, bf16[1024,1024]{1,0:T(8,128)(2,1)}) fusion(f32[1024,1024]{1,0:T(8,128)} %fusion.9, f32[1024]{0:T(1024)S(1)} %bitcast.69, bf16[1024,1024]{1,0:T(8,128)(2,1)S(1)} %bitcast.43, f32[1024,1024]{1,0:T(8,128)} %copy-done.2, f32[1024]{0:T(1024)S(1)} %bitcast.59, f32[1024]{0:T(1024)S(1)} %bitcast.63, ...), kind=kOutput, calls=%fused_computation.48 | convolution fusion | flops 2170551296 | bytes 12603392 | tf_op jit(solution)/shard_map/dot_general | solution.py:61
  93.5 0.0 copy-start.3
  93.5 0.0 copy-start.4
  93.6 2.1 %fusion.4 = f32[2,8,8,128]{3,2,1,0:T(8,128)S(1)} fusion(bf16[16,1024]{1,0:T(8,128)(2,1)S(1)} %copy-done, bf16[1024,1024]{1,0:T(8,128)(2,1)} %get-tuple-element.47), kind=kOutput, calls=%fused_computation.13 | convolution fusion | flops 33554432 | bytes 2195456 | tf_op jit(solution)/shard_map/dot_general | solution.py:66
  97.0 0.3 broadcast_in_dim.36
  97.3 46.1 %all_to_all.11 = f32[8,1,19457]{2,1,0:T(1,128)S(1)} all-to-all(f32[8,1,19457]{2,1,0:T(1,128)S(1)} %broadcast_in_dim.36), channel_id=1, replica_groups=mesh['vol'=64,'path'=8] {'path'}, dimensions={0} | all-to-all | bytes 1245248 | tf_op jit(solution)/shard_map/all_to_all | solution.py:18
  143.5 0.5 reduce_sum.79
  143.9 0.5 slice.88
  145.1 0.6 multiply_subtract_fusion.2
  145.8 0.7 fusion.15
  146.5 12.3 %reduce-scatter.2.cloned.1.call-done = bf16[128,1024]{1,0:T(8,128)(2,1)} async-done(((bf16[1024,1024]{1,0:T(8,128)(2,1)}), bf16[128,1024]{1,0:T(8,128)(2,1)}) %reduce-scatter.2.cloned.1.call-update) | async-done | bytes 262160 | tf_op jit(solution)/shard_map/reduce_scatter | solution.py:130
  158.7 2.1 %fusion.14 = (bf16[1,128,1024]{2,1,0:T(8,128)(2,1)}, f32[1,128,1024]{2,1,0:T(8,128)}, f32[1,128,1024]{2,1,0:T(8,128)}) fusion(f32[1,128,1024]{2,1,0:T(8,128)S(1)} %copy-done.3, bf16[128,1024]{1,0:T(8,128)(2,1)} %reduce-scatter.2.cloned.1.call-done, f32[1,128,1024]{2,1,0:T(8,128)S(1)} %copy-done.4), kind=kLoop, calls=%fused_computation.42 | loop fusion | flops 786432 | bytes 2621440 | tf_op jit(solution)/shard_map/convert_element_type | solution.py:155
  (39 shorter events, 0.2 us)
Async XLA Ops:
  7.2 36.3 %copy-start = (bf16[16,1024]{1,0:T(8,128)(2,1)S(1)}, bf16[16,1024]{1,0:T(8,128)(2,1)}, u32[]{:S(2)}) copy-start(bf16[16,1024]{1,0:T(8,128)(2,1)} %param.13) | copy-start | bytes 98308
  7.2 8.4 %copy-start.13 = (f32[1,1024]{1,0:T(1,128)S(1)}, f32[1,1024]{1,0:T(1,128)}, u32[]{:S(2)}) copy-start(f32[1,1024]{1,0:T(1,128)} %param.15) | copy-start | bytes 12292
  7.2 14.5 %copy-start.10 = (s32[4,2]{0,1:T(2,128)S(1)}, s32[4,2]{0,1:T(2,128)}, u32[]{:S(2)}) copy-start(s32[4,2]{0,1:T(2,128)} %param.17) | copy-start | bytes 100
  7.2 20.9 %copy-start.9 = (f32[4,1024]{1,0:T(4,128)S(1)}, f32[4,1024]{1,0:T(4,128)}, u32[]{:S(2)}) copy-start(f32[4,1024]{1,0:T(4,128)} %param.14) | copy-start | bytes 49156
  7.2 20.9 %copy-start.11 = (s32[3,1,1024]{2,1,0:T(1,128)S(1)}, s32[3,1,1024]{2,1,0:T(1,128)}, u32[]{:S(2)}) copy-start(s32[3,1,1024]{2,1,0:T(1,128)} %param.16) | copy-start | bytes 36868
  7.2 36.2 %copy-start.8 = (bf16[1,16,1024]{2,1,0:T(8,128)(2,1)S(1)}, bf16[1,16,1024]{2,1,0:T(8,128)(2,1)}, u32[]{:S(2)}) copy-start(bf16[1,16,1024]{2,1,0:T(8,128)(2,1)} %param.21) | copy-start | bytes 98308
  9.8 45.4 %copy-start.7 = (f32[1,3,1024]{2,0,1:T(1,128)S(1)}, f32[1,3,1024]{2,0,1:T(1,128)}, u32[]{:S(2)}) copy-start(f32[1,3,1024]{2,0,1:T(1,128)} %param.20) | copy-start | bytes 36868
  9.8 56.7 %all-to-all-start = ((bf16[8,128,1024]{2,1,0:T(8,128)(2,1)}), bf16[8,128,1024]{2,1,0:T(8,128)(2,1)S(1)}, u32[]{:S(2)}, u32[]{:S(2)}) async-start(bf16[8,128,1024]{2,1,0:T(8,128)(2,1)} %stack.15), calls=%async_computation | async-start | bytes 4194304 | tf_op jit(solution)/shard_map/all_to_all | solution.py:84
  15.6 143.2 %reduce-scatter.2.cloned.1.call-start = ((), (), s32[]{:S(2)}) async-start(), calls=%async_computation.3 | async-start | bytes 2359296 | tf_op jit(solution)/shard_map/reduce_scatter | solution.py:130
  15.6 25.0 %collective-permute-start = (f32[1024]{0:T(1024)S(1)}, f32[1024]{0:T(1024)S(1)}, u32[]{:S(2)}, u32[]{:S(2)}) collective-permute-start(f32[1024]{0:T(1024)S(1)} %bitcast.64), channel_id=1, source_target_pairs={{0,8},{8,16},{16,24},{24,32},{32,40},{40,48},{48,56},{56,64},{64,7... | collective-permute-start | bytes 12296 | tf_op jit(solution)/shard_map/ppermute | solution.py:13
  40.6 9.3 %collective-permute-start.1 = (f32[1024]{0:T(1024)S(1)}, f32[1024]{0:T(1024)S(1)}, u32[]{:S(2)}, u32[]{:S(2)}) collective-permute-start(f32[1024]{0:T(1024)S(1)} %multiply_add_fusion.4), channel_id=1, source_target_pairs={{0,8},{8,16},{16,24},{24,32},{32,40},{40,48},{48,56},{56,64},{64,7... | collective-permute-start | bytes 12296 | tf_op jit(solution)/shard_map/ppermute | solution.py:13
  49.9 9.2 %collective-permute-start.2 = (f32[1024]{0:T(1024)S(1)}, f32[1024]{0:T(1024)S(1)}, u32[]{:S(2)}, u32[]{:S(2)}) collective-permute-start(f32[1024]{0:T(1024)S(1)} %multiply_add_fusion.3), channel_id=1, source_target_pairs={{0,8},{8,16},{16,24},{24,32},{32,40},{40,48},{48,56},{56,64},{64,7... | collective-permute-start | bytes 12296 | tf_op jit(solution)/shard_map/ppermute | solution.py:13
  59.6 13.6 %collective-permute-start.3 = (f32[1024]{0:T(1024)S(1)}, f32[1024]{0:T(1024)S(1)}, u32[]{:S(2)}, u32[]{:S(2)}) collective-permute-start(f32[1024]{0:T(1024)S(1)} %get-tuple-element.24), channel_id=1, source_target_pairs={{0,8},{8,16},{16,24},{24,32},{32,40},{40,48},{48,56},{56,64},{64,7... | collective-permute-start | bytes 12296 | tf_op jit(solution)/shard_map/ppermute | solution.py:13
  66.5 8.8 %copy-start.1 = (f32[1024,1024]{1,0:T(8,128)S(1)}, f32[1024,1024]{1,0:T(8,128)}, u32[]{:S(2)}) copy-start(f32[1024,1024]{1,0:T(8,128)} %fusion.9) | copy-start | bytes 12582916
  73.3 2.0 %copy-start.2 = (f32[1024,1024]{1,0:T(8,128)}, f32[1024,1024]{1,0:T(8,128)S(1)}, u32[]{:S(2)}) copy-start(f32[1024,1024]{1,0:T(8,128)S(1)} %get-tuple-element.45) | copy-start | bytes 12582916
  93.5 51.6 %copy-start.12 = (f32[1,3,1024]{2,0,1:T(1,128)S(1)}, f32[1,3,1024]{2,0,1:T(1,128)}, u32[]{:S(2)}) copy-start(f32[1,3,1024]{2,0,1:T(1,128)} %param.25) | copy-start | bytes 36868
  93.5 52.3 %copy-start.5 = (f32[1,16,1024]{2,1,0:T(8,128)S(1)}, f32[1,16,1024]{2,1,0:T(8,128)}, u32[]{:S(2)}) copy-start(f32[1,16,1024]{2,1,0:T(8,128)} %param.18) | copy-start | bytes 196612
  93.5 52.3 %copy-start.6 = (f32[1,16,1024]{2,1,0:T(8,128)S(1)}, f32[1,16,1024]{2,1,0:T(8,128)}, u32[]{:S(2)}) copy-start(f32[1,16,1024]{2,1,0:T(8,128)} %param.23) | copy-start | bytes 196612
  93.5 65.2 %copy-start.3 = (f32[1,128,1024]{2,1,0:T(8,128)S(1)}, f32[1,128,1024]{2,1,0:T(8,128)}, u32[]{:S(2)}) copy-start(f32[1,128,1024]{2,1,0:T(8,128)} %param.19) | copy-start | bytes 1572868
  93.5 65.2 %copy-start.4 = (f32[1,128,1024]{2,1,0:T(8,128)S(1)}, f32[1,128,1024]{2,1,0:T(8,128)}, u32[]{:S(2)}) copy-start(f32[1,128,1024]{2,1,0:T(8,128)} %param.24) | copy-start | bytes 1572868
Sparse Core Ops, SparseCore 0:
  80.7 78.0 reduce-scatter.1
